TPU v7x, 128 devices: a whole 4x4x4 slice. The times are simulated.
128 devices in a mesh: leaf: 16 (over x, y_lo, core), panel: 8 (over z, y_hi).
Axes of the slice: x: 4, y: 4 (y_hi: 2, y_lo: 2; y = y_hi * 2 + y_lo), z: 4, core: 2. Of those that a mesh axis runs over, the one named last changes fastest.
Arguments:
- ext_rows: bfloat16 [16, 4608, 5120], P('leaf', 'panel'), as said below
- iface_rows: bfloat16 [16, 512, 5120], P('leaf', 'panel'), as said below
- inverse: bfloat16 [16, 512, 512], P('leaf', 'panel'), as said below
- pivot: int32 [16, 256], P('leaf'), may hold values from 0 to 255, as said below
- flags: int32 [16, 9], P('leaf'), may hold values 0 or 1
Outputs:
- merged: bfloat16 [16, 4608, 9216], P('leaf', 'panel')
Inputs may be any that keep to these rules, and one draw needn't show every extreme that they name: `pivot`: each row is a permutation of 0 to 255; the rows of two merge partners are inverse to each other. `ext_rows`: each 2 x 2 block of real entries is the real form [[a, -b], [b, a]] of one complex number. `iface_rows`: each 2 x 2 block of real entries is the real form [[a, -b], [b, a]] of one complex number. `inverse`: each 2 x 2 block of real entries is the real form [[a, -b], [b, a]] of one complex number.
All inputs are finite; a program needn't handle non-finite values. No bound on the sum of `flags` on one device may be relied on, other than what follows from the above.
Results may differ from a plain program's by a relative error of at most 0.005.
Values may be sent and summed in bfloat16 or wider, within the bound.
No kernel may reach another device: no remote copies, remote signals or barrier semaphores. Data moves between devices by JAX's collectives and lax.ppermute only.
A program may use at most 128 MiB of HBM per device.

v0:
```python
import functools

import jax
import jax.numpy as jnp
from jax import lax
from jax.experimental import pallas as pl
from jax.experimental.pallas import tpu as pltpu
from jax.sharding import PartitionSpec as P


FPTS = 256
TILE = 768
VMEM_LIMIT = 28 * 2**20
SHIFTS = ((0, 0), (0, 1), (-1, 0), (-1, 1), (1, 0), (1, 1), (2, 0), (2, 1))
F32 = jnp.float32
BF16 = jnp.bfloat16


def kernel_call(body, **kwargs):
    return pl.pallas_call(
        body, compiler_params=pltpu.CompilerParams(vmem_limit_bytes=VMEM_LIMIT), **kwargs
    )


def iota(shape, axis):
    return lax.broadcasted_iota(jnp.int32, shape, axis)


def dot(a, b):
    return jnp.dot(a, b, preferred_element_type=F32)


def row_sign(flags_ref, rows):
    first = lax.axis_index("panel") * rows
    face = (first + iota((rows, 1), 0)) // (2 * FPTS)
    sign = jnp.ones((rows, 1), F32)
    for f in range(flags_ref.shape[1]):
        sign = jnp.where((face == f) & (flags_ref[0, f] == 1), -1.0, sign)
    return sign


def block_index(where, block):
    panel = lax.axis_index("panel")
    z, y = panel // 2, panel % 2
    out = jnp.zeros_like(where)
    for i, (dz, dy) in enumerate(SHIFTS):
        start = (((z + 4 + dz) % 4) * 2 + (y + dy) % 2) * block
        out = jnp.where(where // block == i, start + where % block, out)
    return out


def even_rows(rows):
    return (iota((rows // 2, rows), 1) == 2 * iota((rows // 2, rows), 0)).astype(BF16)


def split_columns(size):
    col = iota((1, size), 1)
    src = jnp.where(col < size // 2, 2 * col, 2 * col - size + 1)
    return (iota((size, size), 0) == src).astype(BF16)


def inward_kernel(iface_ref, inward_ref, held, sem):
    idim = held.shape[1]
    edim = iface_ref.shape[1] - idim
    copy = pltpu.make_async_copy(iface_ref.at[:, pl.ds(edim, idim)], held, sem)
    copy.start()
    deint = split_columns(idim)
    copy.wait()
    inward_ref[...] = dot(dot(even_rows(held.shape[0]), held[...]).astype(BF16), deint).astype(BF16)


def split_kernel(iface_ref, winv_ref, far_ref, own_ref):
    pick = even_rows(iface_ref.shape[0])
    edim = far_ref.shape[1]
    idim = winv_ref.shape[1]
    even = dot(pick, iface_ref[:, :edim]).astype(BF16)
    far_ref[...] = even
    own_ref[:, :edim] = even
    winv = dot(pick, winv_ref[...]).astype(BF16)
    own_ref[:, edim : edim + idim] = dot(winv, split_columns(idim)).astype(BF16)


def prep_kernel(edim, ext_ref, pivot_ref, across_ref, spread_ref, back_ref):
    idim = ext_ref.shape[1] - edim
    half = idim // 2
    block = half // 8
    col = iota((1, idim), 1)
    part = (col >= half).astype(jnp.int32)
    src = 2 * block_index(col - half * part, block) + part
    deint = (iota((idim, idim), 0) == src).astype(BF16)
    pivot = pivot_ref[...]
    spread_ref[...] = (block_index(iota((half, 1), 0), block) == pivot).astype(BF16)
    chosen = (iota((half, half), 0) == block_index(iota((1, half), 1), block)).astype(BF16)
    back_ref[...] = dot((iota((half, half), 0) == pivot).astype(BF16), chosen).astype(BF16)
    across_ref[...] = dot(ext_ref[:, edim:], deint).astype(BF16)


def couple_kernel(edim, flags_ref, across_ref, spread_ref, back_ref, *rest):
    blocks = rest[:8]
    coupled_ref, through_ref = rest[8:]
    rows, idim = across_ref.shape
    half = idim // 2
    gather = lambda at: jnp.concatenate([b[:, at : at + idim] for b in blocks], axis=0)
    spread, back = spread_ref[...], back_ref[...]
    sign = row_sign(flags_ref, rows)

    def times(lhs, even):
        a, nb = even[:, :half], even[:, half:]
        left = dot(lhs[:, :half], a) - dot(lhs[:, half:], nb)
        right = dot(lhs[:, :half], nb) + dot(lhs[:, half:], a)
        return left.astype(BF16), right.astype(BF16)

    nt = lambda v: lax.dot_general(v, spread, (((1,), (1,)), ((), ())), preferred_element_type=F32)
    left, right = times(across_ref[...], gather(edim))
    coupled = jnp.concatenate([nt(left), nt(right)], axis=1)
    left, right = times(coupled.astype(BF16), gather(edim + idim))
    through = jnp.concatenate([dot(left, back), dot(right, back)], axis=1)
    coupled_ref[...] = (coupled * sign).astype(BF16)
    through_ref[...] = (through * sign).astype(BF16)


def product_kernel(edim, at, own, *refs):
    if own:
        flags_ref, lhs_ref, ext_ref, *refs = refs
    else:
        lhs_ref, *refs = refs
    blocks, refs = refs[:8], refs[8:]
    out_ref, held, out_sems = refs[-3:]
    rows, idim = lhs_ref.shape
    wide = 256
    tiles = edim // TILE
    sign = row_sign(flags_ref, rows) if own else None
    is_even = iota((idim // 2, wide), 1) % 2 == 0
    stores = []
    for t in range(tiles):
        for g in range(t * TILE, (t + 1) * TILE, wide):
            cols = slice(g, g + wide)
            even = jnp.concatenate([b[:, cols] for b in blocks], axis=0)
            wider = even.astype(F32)
            odd = jnp.where(is_even, -pltpu.roll(wider, wide - 1, 1), pltpu.roll(wider, 1, 1))
            out = dot(lhs_ref[...], jnp.concatenate([even, odd.astype(BF16)], axis=0))
            if own:
                out += ext_ref[:, cols].astype(F32) * sign
            held[:, cols] = out.astype(BF16)
        store = pltpu.make_async_copy(
            held.at[:, pl.ds(t * TILE, TILE)],
            out_ref.at[:, pl.ds(at + t * TILE, TILE)],
            out_sems.at[t],
        )
        store.start()
        stores.append(store)
    for store in stores:
        store.wait()


def near(array):
    return pltpu.with_memory_space_constraint(array, pltpu.VMEM)


VMEM = pl.BlockSpec(memory_space=pltpu.VMEM)
SMEM = pl.BlockSpec(memory_space=pltpu.SMEM)
ANY = pl.BlockSpec(memory_space=pl.ANY)


def product(lhs, blocks, edim, ext=None, flags=None, out=None):
    rows, idim = lhs.shape
    own = out is None
    tiles = edim // TILE
    if own:
        args = [flags, near(lhs), near(ext), *map(near, blocks)]
        specs = [SMEM] + [VMEM] * 10
        alias = {}
    else:
        args = [near(lhs), *map(near, blocks), out]
        specs = [VMEM] * 9 + [ANY]
        alias = {len(args) - 1: 0}
    scratch = [
        pltpu.VMEM((rows, edim), BF16),
        pltpu.SemaphoreType.DMA((tiles,)),
    ]
    return kernel_call(
        functools.partial(product_kernel, edim, 0 if own else edim, own),
        in_specs=specs,
        out_specs=ANY,
        out_shape=jax.ShapeDtypeStruct((rows, 2 * edim), BF16),
        scratch_shapes=scratch,
        input_output_aliases=alias,
        cost_estimate=pl.CostEstimate(
            flops=2 * rows * idim * edim, transcendentals=0, bytes_accessed=4 * rows * edim
        ),
    )(*args)


def code(x, y, z, c):
    return (((x % 4) * 2 + y % 2) * 2 + c) * 8 + (z % 4) * 2 + (y % 4) // 2


def route(move):
    pairs = []
    for x in range(4):
        for y in range(4):
            for z in range(4):
                for c in range(2):
                    pairs.append((code(x, y, z, c), code(*move(x, y, z), c)))
    return pairs


ROUTES = {
    "x": route(lambda x, y, z: (x ^ 1, y, z)),
    "y": route(lambda x, y, z: (x, y + 2, z)),
    "xy": route(lambda x, y, z: (x ^ 1, y + 2, z)),
    "z+": route(lambda x, y, z: (x, y, z + 1)),
    "z-": route(lambda x, y, z: (x, y, z - 1)),
    "z2": route(lambda x, y, z: (x, y, z + 2)),
}


def send(array, name):
    return lax.ppermute(array, ("leaf", "panel"), ROUTES[name])


def per_device(ext_rows, iface_rows, inverse, pivot, flags):
    return merge(ext_rows[0], iface_rows[0], inverse[0], pivot, flags)[None]


def merge(ext, iface, winv, pivot, flags):
    rows = ext.shape[0]
    idim = winv.shape[1]
    edim = ext.shape[1] - idim
    half = iface.shape[0] // 2
    shape = lambda r, c: jax.ShapeDtypeStruct((r, c), BF16)
    local = lambda r, c: pltpu.VMEM((r, c), BF16)
    inward = kernel_call(
        inward_kernel,
        in_specs=[ANY],
        out_specs=VMEM,
        out_shape=shape(half, idim),
        scratch_shapes=[pltpu.VMEM((2 * half, idim), BF16), pltpu.SemaphoreType.DMA(())],
    )(iface)
    inward = send(inward, "x")
    far, own = kernel_call(
        split_kernel,
        in_specs=[VMEM] * 2,
        out_specs=(VMEM,) * 2,
        out_shape=(local(half, edim), local(half, edim + 2 * idim)),
    )(iface, winv)
    own = lax.dynamic_update_slice(own, inward, (0, edim + idim))
    z2 = send(own, "z2")
    y = send(own, "y")
    x = send(far, "x")
    x_z2 = send(z2, "x")
    y_z2 = send(z2, "y")
    y_zp = send(y, "z+")
    y_zm = send(y, "z-")
    zp = send(own, "z+")
    zm = send(own, "z-")
    xy = send(x, "y")
    x_zp = send(x, "z+")
    x_zm = send(x, "z-")
    xy_zp = send(y_zp, "x")
    xy_z2 = send(x_z2, "y")
    xy_zm = send(y_zm, "x")
    mine = [own, y, zp, y_zp, zm, y_zm, z2, y_z2]
    theirs = [x, xy, x_zp, xy_zp, x_zm, xy_zm, x_z2, xy_z2]
    prep = kernel_call(
        functools.partial(prep_kernel, edim),
        in_specs=[VMEM, VMEM],
        out_specs=(VMEM,) * 3,
        out_shape=(local(rows, idim), local(idim // 2, idim // 2), local(idim // 2, idim // 2)),
    )(near(ext), pivot)
    coupled, through = kernel_call(
        functools.partial(couple_kernel, edim),
        in_specs=[SMEM] + [VMEM] * 11,
        out_specs=(VMEM,) * 2,
        out_shape=(local(rows, idim),) * 2,
    )(flags, *map(near, prep), *map(near, mine))
    out = product(through, mine, edim, ext=ext, flags=flags)
    return product(coupled, theirs, edim, out=out)


def solution(mesh):
    placed = (
        P("leaf", "panel", None),
        P("leaf", "panel", None),
        P("leaf", "panel", None),
        P("leaf", None),
        P("leaf", None),
    )
    return jax.shard_map(
        per_device, mesh=mesh, in_specs=placed, out_specs=P("leaf", "panel", None), check_vma=False
    )
```

profile of v0, /device:TPU:0, one launch (start us, length us, event | category | flops | bytes accessed | tf_op | source)
XLA Modules:
  0.0 60.1 jit_solution(5094901532906955700)
XLA Ops:
  0.0 0.0 copy-start.2
  0.0 1.1 %copy-done.2 = bf16[1,64,5120]{2,1,0:T(8,128)(2,1)S(1)} copy-done((bf16[1,64,5120]{2,1,0:T(8,128)(2,1)S(1)}, bf16[1,64,5120]{2,1,0:T(8,128)(2,1)}, u32[]{:S(2)}) %copy-start.2) | copy-done | bytes 655384
  1.1 0.5 shard_map.57
  1.6 1.7 %collective-permute-start = (bf16[32,512]{1,0:T(8,128)(2,1)S(1)}, bf16[32,512]{1,0:T(8,128)(2,1)S(1)}, u32[]{:S(2)}, u32[]{:S(2)}) collective-permute-start(bf16[32,512]{1,0:T(8,128)(2,1)S(1)} %shard_map.57), channel_id=1, source_target_pairs={{0,32},{8,40},{2,34},{10,42},{4,36},{12,44},{6,38},{14,46},{16,48}... | collective-permute-start | bytes 98312 | tf_op jit(solution)/shard_map/ppermute | solution.py:219
  3.2 0.8 %copy-done.3 = bf16[1,64,512]{2,1,0:T(8,128)(2,1)S(1)} copy-done((bf16[1,64,512]{2,1,0:T(8,128)(2,1)S(1)}, bf16[1,64,512]{2,1,0:T(8,128)(2,1)}, u32[]{:S(2)}) %copy-start.3) | copy-done | bytes 65560
  4.1 0.4 shard_map.56
  4.5 1.1 %collective-permute-done = bf16[32,512]{1,0:T(8,128)(2,1)S(1)} collective-permute-done((bf16[32,512]{1,0:T(8,128)(2,1)S(1)}, bf16[32,512]{1,0:T(8,128)(2,1)S(1)}, u32[]{:S(2)}, u32[]{:S(2)}) %collective-permute-start) | collective-permute-done | bytes 32800 | tf_op jit(solution)/shard_map/ppermute | solution.py:219
  5.6 4.0 %collective-permute-start.6 = (bf16[32,5632]{1,0:T(8,128)(2,1)S(1)}, bf16[32,5632]{1,0:T(8,128)(2,1)S(1)}, u32[]{:S(2)}, u32[]{:S(2)}) collective-permute-start(bf16[32,5632]{1,0:T(8,128)(2,1)S(1)} %constant_dynamic-update-slice_fusion.rest_0_.refs_3_), channel_id=1, source_target_pairs={{0,4},{8,12},{2,6},{10,14},{4,0},{12,8},{6,2},{14,10},{16,20},{24,... | collective-permute-start | bytes 1081352 | tf_op jit(solution)/shard_map/ppermute | solution.py:219
  9.5 3.2 %collective-permute-start.1 = (bf16[32,5632]{1,0:T(8,128)(2,1)S(1)}, bf16[32,5632]{1,0:T(8,128)(2,1)S(1)}, u32[]{:S(2)}, u32[]{:S(2)}) collective-permute-start(bf16[32,5632]{1,0:T(8,128)(2,1)S(1)} %constant_dynamic-update-slice_fusion.rest_0_.refs_3_), channel_id=1, source_target_pairs={{0,1},{8,9},{2,3},{10,11},{4,5},{12,13},{6,7},{14,15},{16,17},{24,... | collective-permute-start | bytes 1081352 | tf_op jit(solution)/shard_map/ppermute | solution.py:219
  12.7 0.7 %collective-permute-start.4 = (bf16[32,5632]{1,0:T(8,128)(2,1)S(1)}, bf16[32,5632]{1,0:T(8,128)(2,1)S(1)}, u32[]{:S(2)}, u32[]{:S(2)}) collective-permute-start(bf16[32,5632]{1,0:T(8,128)(2,1)S(1)} %constant_dynamic-update-slice_fusion.rest_0_.refs_3_), channel_id=1, source_target_pairs={{0,6},{8,14},{2,0},{10,8},{4,2},{12,10},{6,4},{14,12},{16,22},{24,... | collective-permute-start | bytes 1081352 | tf_op jit(solution)/shard_map/ppermute | solution.py:219
  13.4 1.5 %collective-permute-start.8 = (bf16[32,4608]{1,0:T(8,128)(2,1)S(1)}, bf16[32,4608]{1,0:T(8,128)(2,1)S(1)}, u32[]{:S(2)}, u32[]{:S(2)}) collective-permute-start(bf16[32,4608]{1,0:T(8,128)(2,1)S(1)} %get-tuple-element.17), channel_id=1, source_target_pairs={{0,32},{8,40},{2,34},{10,42},{4,36},{12,44},{6,38},{14,46},{16,48}... | collective-permute-start | bytes 884744 | tf_op jit(solution)/shard_map/ppermute | solution.py:219
  14.9 1.3 %collective-permute-start.2 = (bf16[32,5632]{1,0:T(8,128)(2,1)S(1)}, bf16[32,5632]{1,0:T(8,128)(2,1)S(1)}, u32[]{:S(2)}, u32[]{:S(2)}) collective-permute-start(bf16[32,5632]{1,0:T(8,128)(2,1)S(1)} %constant_dynamic-update-slice_fusion.rest_0_.refs_3_), channel_id=1, source_target_pairs={{0,2},{8,10},{2,4},{10,12},{4,6},{12,14},{6,0},{14,8},{16,18},{24,... | collective-permute-start | bytes 1081352 | tf_op jit(solution)/shard_map/ppermute | solution.py:219
  16.3 1.9 %collective-permute-done.6.rest_6_.refs_9_ = bf16[32,5632]{1,0:T(8,128)(2,1)S(1)} collective-permute-done((bf16[32,5632]{1,0:T(8,128)(2,1)S(1)}, bf16[32,5632]{1,0:T(8,128)(2,1)S(1)}, u32[]{:S(2)}, u32[]{:S(2)}) %collective-permute-start.6) | collective-permute-done | bytes 360480 | tf_op jit(solution)/shard_map/ppermute | solution.py:219
  18.2 2.1 %collective-permute-start.14 = (bf16[32,5632]{1,0:T(8,128)(2,1)S(1)}, bf16[32,5632]{1,0:T(8,128)(2,1)S(1)}, u32[]{:S(2)}, u32[]{:S(2)}) collective-permute-start(bf16[32,5632]{1,0:T(8,128)(2,1)S(1)} %collective-permute-done.6.rest_6_.refs_9_), channel_id=1, source_target_pairs={{0,32},{8,40},{2,34},{10,42},{4,36},{12,44},{6,38},{14,46},{16,48}... | collective-permute-start | bytes 1081352 | tf_op jit(solution)/shard_map/ppermute | solution.py:219
  20.3 0.0 collective-permute-done.1.rest_1_.refs_4_
  20.3 3.7 %collective-permute-start.5 = (bf16[32,5632]{1,0:T(8,128)(2,1)S(1)}, bf16[32,5632]{1,0:T(8,128)(2,1)S(1)}, u32[]{:S(2)}, u32[]{:S(2)}) collective-permute-start(bf16[32,5632]{1,0:T(8,128)(2,1)S(1)} %collective-permute-done.1.rest_1_.refs_4_), channel_id=1, source_target_pairs={{0,6},{8,14},{2,0},{10,8},{4,2},{12,10},{6,4},{14,12},{16,22},{24,... | collective-permute-start | bytes 1081352 | tf_op jit(solution)/shard_map/ppermute | solution.py:219
  24.0 0.0 collective-permute-done.8.refs_1_
  24.0 0.5 collective-permute-start.3
  24.5 3.1 %collective-permute-done.4.rest_4_.refs_7_ = bf16[32,5632]{1,0:T(8,128)(2,1)S(1)} collective-permute-done((bf16[32,5632]{1,0:T(8,128)(2,1)S(1)}, bf16[32,5632]{1,0:T(8,128)(2,1)S(1)}, u32[]{:S(2)}, u32[]{:S(2)}) %collective-permute-start.4) | collective-permute-done | bytes 360480 | tf_op jit(solution)/shard_map/ppermute | solution.py:219
  27.6 3.2 %collective-permute-start.7 = (bf16[32,5632]{1,0:T(8,128)(2,1)S(1)}, bf16[32,5632]{1,0:T(8,128)(2,1)S(1)}, u32[]{:S(2)}, u32[]{:S(2)}) collective-permute-start(bf16[32,5632]{1,0:T(8,128)(2,1)S(1)} %collective-permute-done.6.rest_6_.refs_9_), channel_id=1, source_target_pairs={{0,1},{8,9},{2,3},{10,11},{4,5},{12,13},{6,7},{14,15},{16,17},{24,... | collective-permute-start | bytes 1081352 | tf_op jit(solution)/shard_map/ppermute | solution.py:219
  30.7 0.0 collective-permute-done.2.rest_2_.refs_5_
  30.7 0.5 collective-permute-start.12
  31.2 0.0 collective-permute-done.14.refs_7_
  31.2 0.4 collective-permute-start.15
  31.6 3.7 %collective-permute-done.5.rest_5_.refs_8_ = bf16[32,5632]{1,0:T(8,128)(2,1)S(1)} collective-permute-done((bf16[32,5632]{1,0:T(8,128)(2,1)S(1)}, bf16[32,5632]{1,0:T(8,128)(2,1)S(1)}, u32[]{:S(2)}, u32[]{:S(2)}) %collective-permute-start.5) | collective-permute-done | bytes 360480 | tf_op jit(solution)/shard_map/ppermute | solution.py:219
  35.3 1.5 %collective-permute-start.13 = (bf16[32,5632]{1,0:T(8,128)(2,1)S(1)}, bf16[32,5632]{1,0:T(8,128)(2,1)S(1)}, u32[]{:S(2)}, u32[]{:S(2)}) collective-permute-start(bf16[32,5632]{1,0:T(8,128)(2,1)S(1)} %collective-permute-done.5.rest_5_.refs_8_), channel_id=1, source_target_pairs={{0,32},{8,40},{2,34},{10,42},{4,36},{12,44},{6,38},{14,46},{16,48}... | collective-permute-start | bytes 1081352 | tf_op jit(solution)/shard_map/ppermute | solution.py:219
  36.8 0.0 collective-permute-done.3.rest_3_.refs_6_
  36.8 0.5 collective-permute-start.11
  37.3 2.0 %collective-permute-done.12.refs_5_ = bf16[32,4608]{1,0:T(8,128)(2,1)S(1)} collective-permute-done((bf16[32,4608]{1,0:T(8,128)(2,1)S(1)}, bf16[32,4608]{1,0:T(8,128)(2,1)S(1)}, u32[]{:S(2)}, u32[]{:S(2)}) %collective-permute-start.12) | collective-permute-done | bytes 294944 | tf_op jit(solution)/shard_map/ppermute | solution.py:219
  39.3 0.5 collective-permute-start.10
  39.9 0.0 collective-permute-done.7.rest_7_.refs_10_
  39.9 3.3 %collective-permute-start.9 = (bf16[32,4608]{1,0:T(8,128)(2,1)S(1)}, bf16[32,4608]{1,0:T(8,128)(2,1)S(1)}, u32[]{:S(2)}, u32[]{:S(2)}) collective-permute-start(bf16[32,4608]{1,0:T(8,128)(2,1)S(1)} %collective-permute-done.8.refs_1_), channel_id=1, source_target_pairs={{0,1},{8,9},{2,3},{10,11},{4,5},{12,13},{6,7},{14,15},{16,17},{24,... | collective-permute-start | bytes 884744 | tf_op jit(solution)/shard_map/ppermute | solution.py:219
  43.1 0.0 copy-start
  43.1 2.7 %copy-done = bf16[1,576,5120]{2,1,0:T(8,128)(2,1)S(1)} copy-done((bf16[1,576,5120]{2,1,0:T(8,128)(2,1)S(1)}, bf16[1,576,5120]{2,1,0:T(8,128)(2,1)}, u32[]{:S(2)}) %copy-start) | copy-done | bytes 5898264
  45.8 0.0 copy-start.5
  45.8 0.7 %copy-done.5 = s32[1,256]{1,0:T(1,128)S(1)} copy-done((s32[1,256]{1,0:T(1,128)S(1)}, s32[1,256]{1,0:T(1,128)}, u32[]{:S(2)}) %copy-start.5) | copy-done | bytes 1048
  46.5 0.6 %shard_map.55 = (bf16[576,512]{1,0:T(8,128)(2,1)S(1)}, bf16[256,256]{1,0:T(8,128)(2,1)S(1)}, bf16[256,256]{1,0:T(8,128)(2,1)S(1)}) custom-call(bf16[576,5120]{1,0:T(8,128)(2,1)S(1)} %bitcast.4, s32[1,256]{1,0:T(1,128)S(1)} %copy-done.5), custom_call_target="tpu_custom_call" | custom-call | tf_op jit(solution)/shard_map/pallas_call | solution.py:265
  47.1 0.0 copy-start.4
  47.1 0.9 %copy-done.4 = s32[1,9]{1,0:T(1,128)S(1)} copy-done((s32[1,9]{1,0:T(1,128)S(1)}, s32[1,9]{1,0:T(1,128)}, u32[]{:S(2)}) %copy-start.4) | copy-done | bytes 60
  48.0 2.0 %shard_map.58 = (bf16[576,512]{1,0:T(8,128)(2,1)S(1)}, bf16[576,512]{1,0:T(8,128)(2,1)S(1)}) custom-call(s32[1,9]{1,0:T(1,128)S(1)} %copy-done.4, bf16[576,512]{1,0:T(8,128)(2,1)S(1)} %get-tuple-element.12.across_ref, bf16[256,256]{1,0:T(8,128)(2,1)S(1)} %get-tuple-element.13.spread_ref, bf16[256,256]{1,0:T(8,128)(2,1)S(1)} %get-tuple-element.14.back_ref, ...), custom_call_target="tpu_custom_call" | custom-call | tf_op jit(solution)/shard_map/pallas_call | solution.py:271
  50.0 0.0 copy-done.1
  50.1 5.7 %shard_map.59.refs_9_ = bf16[576,9216]{1,0:T(8,128)(2,1)} custom-call(s32[1,9]{1,0:T(1,128)S(1)} %copy-done.4, bf16[576,512]{1,0:T(8,128)(2,1)S(1)} %get-tuple-element.18.refs_1_, bf16[576,5120]{1,0:T(8,128)(2,1)S(1)} %bitcast.5, bf16[32,5632]{1,0:T(8,128)(2,1)S(1)} %constant_dynamic-update-slice_fusion.rest_0_.refs_3_, ...), custom_call_target="tpu_custom_call" | custom-call | flops 2717908992 | bytes 10616832 | tf_op jit(solution)/shard_map/pallas_call | solution.py:181
  55.8 0.0 collective-permute-done.10.refs_3_
  55.8 0.0 collective-permute-done.9.refs_2_
  55.8 0.0 collective-permute-done.15.refs_8_
  55.8 0.0 collective-permute-done.13.refs_6_
  55.8 0.0 collective-permute-done.11.refs_4_
  55.8 4.1 %shard_map.60 = bf16[576,9216]{1,0:T(8,128)(2,1)} custom-call(bf16[576,512]{1,0:T(8,128)(2,1)S(1)} %get-tuple-element.16.refs_0_, bf16[32,4608]{1,0:T(8,128)(2,1)S(1)} %collective-permute-done.8.refs_1_, bf16[32,4608]{1,0:T(8,128)(2,1)S(1)} %collective-permute-done.9.refs_2_, ...), custom_call_target="tpu_custom_call", output_to_operand_aliasing={{}: (9, {})} | custom-call | flops 2717908992 | bytes 10616832 | tf_op jit(solution)/shard_map/pallas_call | solution.py:181
  (3 shorter events, 0.0 us)
Async XLA Ops:
  0.0 1.1 %copy-start.2 = (bf16[1,64,5120]{2,1,0:T(8,128)(2,1)S(1)}, bf16[1,64,5120]{2,1,0:T(8,128)(2,1)}, u32[]{:S(2)}) copy-start(bf16[1,64,5120]{2,1,0:T(8,128)(2,1)} %param.6) | copy-start | bytes 1966084
  1.6 4.0 %collective-permute-start = (bf16[32,512]{1,0:T(8,128)(2,1)S(1)}, bf16[32,512]{1,0:T(8,128)(2,1)S(1)}, u32[]{:S(2)}, u32[]{:S(2)}) collective-permute-start(bf16[32,512]{1,0:T(8,128)(2,1)S(1)} %shard_map.57), channel_id=1, source_target_pairs={{0,32},{8,40},{2,34},{10,42},{4,36},{12,44},{6,38},{14,46},{16,48}... | collective-permute-start | bytes 98312 | tf_op jit(solution)/shard_map/ppermute | solution.py:219
  3.2 0.8 %copy-start.3 = (bf16[1,64,512]{2,1,0:T(8,128)(2,1)S(1)}, bf16[1,64,512]{2,1,0:T(8,128)(2,1)}, u32[]{:S(2)}) copy-start(bf16[1,64,512]{2,1,0:T(8,128)(2,1)} %param.7) | copy-start | bytes 196612
  5.6 12.6 %collective-permute-start.6 = (bf16[32,5632]{1,0:T(8,128)(2,1)S(1)}, bf16[32,5632]{1,0:T(8,128)(2,1)S(1)}, u32[]{:S(2)}, u32[]{:S(2)}) collective-permute-start(bf16[32,5632]{1,0:T(8,128)(2,1)S(1)} %constant_dynamic-update-slice_fusion.rest_0_.refs_3_), channel_id=1, source_target_pairs={{0,4},{8,12},{2,6},{10,14},{4,0},{12,8},{6,2},{14,10},{16,20},{24,... | collective-permute-start | bytes 1081352 | tf_op jit(solution)/shard_map/ppermute | solution.py:219
  9.5 10.8 %collective-permute-start.1 = (bf16[32,5632]{1,0:T(8,128)(2,1)S(1)}, bf16[32,5632]{1,0:T(8,128)(2,1)S(1)}, u32[]{:S(2)}, u32[]{:S(2)}) collective-permute-start(bf16[32,5632]{1,0:T(8,128)(2,1)S(1)} %constant_dynamic-update-slice_fusion.rest_0_.refs_3_), channel_id=1, source_target_pairs={{0,1},{8,9},{2,3},{10,11},{4,5},{12,13},{6,7},{14,15},{16,17},{24,... | collective-permute-start | bytes 1081352 | tf_op jit(solution)/shard_map/ppermute | solution.py:219
  12.7 14.8 %collective-permute-start.4 = (bf16[32,5632]{1,0:T(8,128)(2,1)S(1)}, bf16[32,5632]{1,0:T(8,128)(2,1)S(1)}, u32[]{:S(2)}, u32[]{:S(2)}) collective-permute-start(bf16[32,5632]{1,0:T(8,128)(2,1)S(1)} %constant_dynamic-update-slice_fusion.rest_0_.refs_3_), channel_id=1, source_target_pairs={{0,6},{8,14},{2,0},{10,8},{4,2},{12,10},{6,4},{14,12},{16,22},{24,... | collective-permute-start | bytes 1081352 | tf_op jit(solution)/shard_map/ppermute | solution.py:219
  13.4 10.6 %collective-permute-start.8 = (bf16[32,4608]{1,0:T(8,128)(2,1)S(1)}, bf16[32,4608]{1,0:T(8,128)(2,1)S(1)}, u32[]{:S(2)}, u32[]{:S(2)}) collective-permute-start(bf16[32,4608]{1,0:T(8,128)(2,1)S(1)} %get-tuple-element.17), channel_id=1, source_target_pairs={{0,32},{8,40},{2,34},{10,42},{4,36},{12,44},{6,38},{14,46},{16,48}... | collective-permute-start | bytes 884744 | tf_op jit(solution)/shard_map/ppermute | solution.py:219
  14.9 15.8 %collective-permute-start.2 = (bf16[32,5632]{1,0:T(8,128)(2,1)S(1)}, bf16[32,5632]{1,0:T(8,128)(2,1)S(1)}, u32[]{:S(2)}, u32[]{:S(2)}) collective-permute-start(bf16[32,5632]{1,0:T(8,128)(2,1)S(1)} %constant_dynamic-update-slice_fusion.rest_0_.refs_3_), channel_id=1, source_target_pairs={{0,2},{8,10},{2,4},{10,12},{4,6},{12,14},{6,0},{14,8},{16,18},{24,... | collective-permute-start | bytes 1081352 | tf_op jit(solution)/shard_map/ppermute | solution.py:219
  18.2 13.0 %collective-permute-start.14 = (bf16[32,5632]{1,0:T(8,128)(2,1)S(1)}, bf16[32,5632]{1,0:T(8,128)(2,1)S(1)}, u32[]{:S(2)}, u32[]{:S(2)}) collective-permute-start(bf16[32,5632]{1,0:T(8,128)(2,1)S(1)} %collective-permute-done.6.rest_6_.refs_9_), channel_id=1, source_target_pairs={{0,32},{8,40},{2,34},{10,42},{4,36},{12,44},{6,38},{14,46},{16,48}... | collective-permute-start | bytes 1081352 | tf_op jit(solution)/shard_map/ppermute | solution.py:219
  20.3 15.0 %collective-permute-start.5 = (bf16[32,5632]{1,0:T(8,128)(2,1)S(1)}, bf16[32,5632]{1,0:T(8,128)(2,1)S(1)}, u32[]{:S(2)}, u32[]{:S(2)}) collective-permute-start(bf16[32,5632]{1,0:T(8,128)(2,1)S(1)} %collective-permute-done.1.rest_1_.refs_4_), channel_id=1, source_target_pairs={{0,6},{8,14},{2,0},{10,8},{4,2},{12,10},{6,4},{14,12},{16,22},{24,... | collective-permute-start | bytes 1081352 | tf_op jit(solution)/shard_map/ppermute | solution.py:219
  24.0 12.8 %collective-permute-start.3 = (bf16[32,5632]{1,0:T(8,128)(2,1)S(1)}, bf16[32,5632]{1,0:T(8,128)(2,1)S(1)}, u32[]{:S(2)}, u32[]{:S(2)}) collective-permute-start(bf16[32,5632]{1,0:T(8,128)(2,1)S(1)} %collective-permute-done.1.rest_1_.refs_4_), channel_id=1, source_target_pairs={{0,2},{8,10},{2,4},{10,12},{4,6},{12,14},{6,0},{14,8},{16,18},{24,... | collective-permute-start | bytes 1081352 | tf_op jit(solution)/shard_map/ppermute | solution.py:219
  27.6 12.3 %collective-permute-start.7 = (bf16[32,5632]{1,0:T(8,128)(2,1)S(1)}, bf16[32,5632]{1,0:T(8,128)(2,1)S(1)}, u32[]{:S(2)}, u32[]{:S(2)}) collective-permute-start(bf16[32,5632]{1,0:T(8,128)(2,1)S(1)} %collective-permute-done.6.rest_6_.refs_9_), channel_id=1, source_target_pairs={{0,1},{8,9},{2,3},{10,11},{4,5},{12,13},{6,7},{14,15},{16,17},{24,... | collective-permute-start | bytes 1081352 | tf_op jit(solution)/shard_map/ppermute | solution.py:219
  30.7 8.6 %collective-permute-start.12 = (bf16[32,4608]{1,0:T(8,128)(2,1)S(1)}, bf16[32,4608]{1,0:T(8,128)(2,1)S(1)}, u32[]{:S(2)}, u32[]{:S(2)}) collective-permute-start(bf16[32,4608]{1,0:T(8,128)(2,1)S(1)} %collective-permute-done.8.refs_1_), channel_id=1, source_target_pairs={{0,6},{8,14},{2,0},{10,8},{4,2},{12,10},{6,4},{14,12},{16,22},{24,... | collective-permute-start | bytes 884744 | tf_op jit(solution)/shard_map/ppermute | solution.py:219
  31.2 24.6 %collective-permute-start.15 = (bf16[32,5632]{1,0:T(8,128)(2,1)S(1)}, bf16[32,5632]{1,0:T(8,128)(2,1)S(1)}, u32[]{:S(2)}, u32[]{:S(2)}) collective-permute-start(bf16[32,5632]{1,0:T(8,128)(2,1)S(1)} %collective-permute-done.14.refs_7_), channel_id=1, source_target_pairs={{0,1},{8,9},{2,3},{10,11},{4,5},{12,13},{6,7},{14,15},{16,17},{24,... | collective-permute-start | bytes 1081352 | tf_op jit(solution)/shard_map/ppermute | solution.py:219
  35.3 20.5 %collective-permute-start.13 = (bf16[32,5632]{1,0:T(8,128)(2,1)S(1)}, bf16[32,5632]{1,0:T(8,128)(2,1)S(1)}, u32[]{:S(2)}, u32[]{:S(2)}) collective-permute-start(bf16[32,5632]{1,0:T(8,128)(2,1)S(1)} %collective-permute-done.5.rest_5_.refs_8_), channel_id=1, source_target_pairs={{0,32},{8,40},{2,34},{10,42},{4,36},{12,44},{6,38},{14,46},{16,48}... | collective-permute-start | bytes 1081352 | tf_op jit(solution)/shard_map/ppermute | solution.py:219
  36.8 19.0 %collective-permute-start.11 = (bf16[32,5632]{1,0:T(8,128)(2,1)S(1)}, bf16[32,5632]{1,0:T(8,128)(2,1)S(1)}, u32[]{:S(2)}, u32[]{:S(2)}) collective-permute-start(bf16[32,5632]{1,0:T(8,128)(2,1)S(1)} %collective-permute-done.3.rest_3_.refs_6_), channel_id=1, source_target_pairs={{0,32},{8,40},{2,34},{10,42},{4,36},{12,44},{6,38},{14,46},{16,48}... | collective-permute-start | bytes 1081352 | tf_op jit(solution)/shard_map/ppermute | solution.py:219
  39.3 16.4 %collective-permute-start.10 = (bf16[32,4608]{1,0:T(8,128)(2,1)S(1)}, bf16[32,4608]{1,0:T(8,128)(2,1)S(1)}, u32[]{:S(2)}, u32[]{:S(2)}) collective-permute-start(bf16[32,4608]{1,0:T(8,128)(2,1)S(1)} %collective-permute-done.8.refs_1_), channel_id=1, source_target_pairs={{0,2},{8,10},{2,4},{10,12},{4,6},{12,14},{6,0},{14,8},{16,18},{24,... | collective-permute-start | bytes 884744 | tf_op jit(solution)/shard_map/ppermute | solution.py:219
  39.9 15.9 %collective-permute-start.9 = (bf16[32,4608]{1,0:T(8,128)(2,1)S(1)}, bf16[32,4608]{1,0:T(8,128)(2,1)S(1)}, u32[]{:S(2)}, u32[]{:S(2)}) collective-permute-start(bf16[32,4608]{1,0:T(8,128)(2,1)S(1)} %collective-permute-done.8.refs_1_), channel_id=1, source_target_pairs={{0,1},{8,9},{2,3},{10,11},{4,5},{12,13},{6,7},{14,15},{16,17},{24,... | collective-permute-start | bytes 884744 | tf_op jit(solution)/shard_map/ppermute | solution.py:219
  43.1 2.7 %copy-start = (bf16[1,576,5120]{2,1,0:T(8,128)(2,1)S(1)}, bf16[1,576,5120]{2,1,0:T(8,128)(2,1)}, u32[]{:S(2)}) copy-start(bf16[1,576,5120]{2,1,0:T(8,128)(2,1)} %param.5) | copy-start | bytes 17694724
  45.8 0.7 %copy-start.5 = (s32[1,256]{1,0:T(1,128)S(1)}, s32[1,256]{1,0:T(1,128)}, u32[]{:S(2)}) copy-start(s32[1,256]{1,0:T(1,128)} %pivot_ref.1) | copy-start | bytes 3076
  46.5 3.6 %copy-start.1 = (bf16[1,576,5120]{2,1,0:T(8,128)(2,1)S(1)}, bf16[1,576,5120]{2,1,0:T(8,128)(2,1)}, u32[]{:S(2)}) copy-start(bf16[1,576,5120]{2,1,0:T(8,128)(2,1)} %param.5) | copy-start | bytes 17694724
  47.1 0.9 %copy-start.4 = (s32[1,9]{1,0:T(1,128)S(1)}, s32[1,9]{1,0:T(1,128)}, u32[]{:S(2)}) copy-start(s32[1,9]{1,0:T(1,128)} %refs_0_.1) | copy-start | bytes 112
where the time goes:
time: 60.6 us; the launch traced here: 60.1 us
  starting transfers between devices  28.6 us (47%)
  Pallas kernels  13.3 us (22%)
  waiting for transfers between devices  11.8 us (19%)
  local copies, waits for them, and re-layouts  6.21 us (10%)
    ppermute x16, starting transfers between devices, send(): return lax.ppermute(array, ('leaf', 'panel'), ROUTES[name])  28.6 us
    ppermute x16, waiting for transfers between devices, send(): return lax.ppermute(array, ('leaf', 'panel'), ROUTES[name])  11.8 us
    pallas_call x2, Pallas kernels, product(): kernel_call(functools.partial(product_kernel, edim, 0 if own else edim, o...  9.83 us
    unnamed x12, local copies, waits for them, and re-layouts  6.21 us
    pallas_call x1, Pallas kernels, merge(): kernel_call(functools.partial(couple_kernel, edim), in_specs=[SMEM] + [VM...  2 us
  transfers between devices with their start and end apart: 16, of which 5 were waited for; matrix products, arithmetic and copies ran while one was open for 0% of the time, Pallas kernels for 15%

commit v1 on v0

--- a/solution.py
+++ b/solution.py
@@ -9,7 +9,7 @@
 
 
 FPTS = 256
-TILE = 768
+TILE = 512
 VMEM_LIMIT = 28 * 2**20
 SHIFTS = ((0, 0), (0, 1), (-1, 0), (-1, 1), (1, 0), (1, 1), (2, 0), (2, 1))
 F32 = jnp.float32
@@ -17,9 +17,8 @@
 
 
 def kernel_call(body, **kwargs):
-    return pl.pallas_call(
-        body, compiler_params=pltpu.CompilerParams(vmem_limit_bytes=VMEM_LIMIT), **kwargs
-    )
+    params = pltpu.CompilerParams(vmem_limit_bytes=VMEM_LIMIT)
+    return pl.pallas_call(body, compiler_params=params, **kwargs)
 
 
 def iota(shape, axis):
@@ -69,40 +68,58 @@
     inward_ref[...] = dot(dot(even_rows(held.shape[0]), held[...]).astype(BF16), deint).astype(BF16)
 
 
-def split_kernel(iface_ref, winv_ref, far_ref, own_ref):
-    pick = even_rows(iface_ref.shape[0])
+def split_kernel(iface_hbm, winv_hbm, far_ref, own_ref, iface_ref, winv_ref, sems):
     edim = far_ref.shape[1]
     idim = winv_ref.shape[1]
-    even = dot(pick, iface_ref[:, :edim]).astype(BF16)
+    wide = pltpu.make_async_copy(iface_hbm.at[:, pl.ds(0, edim)], iface_ref, sems.at[0])
+    wide.start()
+    square = pltpu.make_async_copy(winv_hbm, winv_ref, sems.at[1])
+    square.start()
+    pick = even_rows(iface_ref.shape[0])
+    wide.wait()
+    even = dot(pick, iface_ref[...]).astype(BF16)
     far_ref[...] = even
     own_ref[:, :edim] = even
+    square.wait()
     winv = dot(pick, winv_ref[...]).astype(BF16)
     own_ref[:, edim : edim + idim] = dot(winv, split_columns(idim)).astype(BF16)
 
 
-def prep_kernel(edim, ext_ref, pivot_ref, across_ref, spread_ref, back_ref):
-    idim = ext_ref.shape[1] - edim
+def prep_kernel(edim, flags_hbm, ext_hbm, pivot_hbm, *refs):
+    across_ref, spread_ref, back_ref, sign_ref, held, pivot_ref, flags_ref, sems = refs
+    idim = held.shape[1]
+    loads = [
+        pltpu.make_async_copy(pivot_hbm, pivot_ref, sems.at[0]),
+        pltpu.make_async_copy(flags_hbm, flags_ref, sems.at[1]),
+        pltpu.make_async_copy(ext_hbm.at[:, pl.ds(edim, idim)], held, sems.at[2]),
+    ]
+    for load in loads:
+        load.start()
     half = idim // 2
     block = half // 8
     col = iota((1, idim), 1)
     part = (col >= half).astype(jnp.int32)
     src = 2 * block_index(col - half * part, block) + part
     deint = (iota((idim, idim), 0) == src).astype(BF16)
+    loads[0].wait()
     pivot = pivot_ref[...]
     spread_ref[...] = (block_index(iota((half, 1), 0), block) == pivot).astype(BF16)
     chosen = (iota((half, half), 0) == block_index(iota((1, half), 1), block)).astype(BF16)
     back_ref[...] = dot((iota((half, half), 0) == pivot).astype(BF16), chosen).astype(BF16)
-    across_ref[...] = dot(ext_ref[:, edim:], deint).astype(BF16)
-
-
-def couple_kernel(edim, flags_ref, across_ref, spread_ref, back_ref, *rest):
+    loads[1].wait()
+    sign_ref[...] = jnp.broadcast_to(row_sign(flags_ref, sign_ref.shape[0]), sign_ref.shape)
+    loads[2].wait()
+    across_ref[...] = dot(held[...], deint).astype(BF16)
+
+
+def couple_kernel(edim, across_ref, spread_ref, back_ref, sign_ref, *rest):
     blocks = rest[:8]
     coupled_ref, through_ref = rest[8:]
-    rows, idim = across_ref.shape
+    _, idim = across_ref.shape
     half = idim // 2
     gather = lambda at: jnp.concatenate([b[:, at : at + idim] for b in blocks], axis=0)
     spread, back = spread_ref[...], back_ref[...]
-    sign = row_sign(flags_ref, rows)
+    sign = sign_ref[:, :1]
 
     def times(lhs, even):
         a, nb = even[:, :half], even[:, half:]
@@ -121,15 +138,15 @@
 
 def product_kernel(edim, at, own, *refs):
     if own:
-        flags_ref, lhs_ref, ext_ref, *refs = refs
+        sign_ref, lhs_ref, ext_ref, *refs = refs
     else:
         lhs_ref, *refs = refs
     blocks, refs = refs[:8], refs[8:]
     out_ref, held, out_sems = refs[-3:]
-    rows, idim = lhs_ref.shape
+    _, idim = lhs_ref.shape
     wide = 256
     tiles = edim // TILE
-    sign = row_sign(flags_ref, rows) if own else None
+    sign = sign_ref[:, :1] if own else None
     is_even = iota((idim // 2, wide), 1) % 2 == 0
     stores = []
     for t in range(tiles):
@@ -153,6 +170,10 @@
         store.wait()
 
 
+def distant(array):
+    return pltpu.with_memory_space_constraint(array, pltpu.HBM)
+
+
 def near(array):
     return pltpu.with_memory_space_constraint(array, pltpu.VMEM)
 
@@ -160,15 +181,16 @@
 VMEM = pl.BlockSpec(memory_space=pltpu.VMEM)
 SMEM = pl.BlockSpec(memory_space=pltpu.SMEM)
 ANY = pl.BlockSpec(memory_space=pl.ANY)
-
-
-def product(lhs, blocks, edim, ext=None, flags=None, out=None):
+HBM = pl.BlockSpec(memory_space=pltpu.HBM)
+
+
+def product(lhs, blocks, edim, ext=None, sign=None, out=None):
     rows, idim = lhs.shape
     own = out is None
     tiles = edim // TILE
     if own:
-        args = [flags, near(lhs), near(ext), *map(near, blocks)]
-        specs = [SMEM] + [VMEM] * 10
+        args = [near(sign), near(lhs), near(ext), *map(near, blocks)]
+        specs = [VMEM] * 11
         alias = {}
     else:
         args = [near(lhs), *map(near, blocks), out]
@@ -228,53 +250,68 @@
     idim = winv.shape[1]
     edim = ext.shape[1] - idim
     half = iface.shape[0] // 2
-    shape = lambda r, c: jax.ShapeDtypeStruct((r, c), BF16)
     local = lambda r, c: pltpu.VMEM((r, c), BF16)
     inward = kernel_call(
         inward_kernel,
-        in_specs=[ANY],
+        in_specs=[HBM],
         out_specs=VMEM,
-        out_shape=shape(half, idim),
+        out_shape=local(half, idim),
         scratch_shapes=[pltpu.VMEM((2 * half, idim), BF16), pltpu.SemaphoreType.DMA(())],
-    )(iface)
+    )(distant(iface))
     inward = send(inward, "x")
     far, own = kernel_call(
         split_kernel,
-        in_specs=[VMEM] * 2,
+        in_specs=[HBM] * 2,
         out_specs=(VMEM,) * 2,
         out_shape=(local(half, edim), local(half, edim + 2 * idim)),
-    )(iface, winv)
+        scratch_shapes=[
+            pltpu.VMEM((2 * half, edim), BF16),
+            pltpu.VMEM((2 * half, idim), BF16),
+            pltpu.SemaphoreType.DMA((2,)),
+        ],
+    )(distant(iface), distant(winv))
     own = lax.dynamic_update_slice(own, inward, (0, edim + idim))
     z2 = send(own, "z2")
     y = send(own, "y")
     x = send(far, "x")
-    x_z2 = send(z2, "x")
-    y_z2 = send(z2, "y")
-    y_zp = send(y, "z+")
-    y_zm = send(y, "z-")
     zp = send(own, "z+")
     zm = send(own, "z-")
     xy = send(x, "y")
-    x_zp = send(x, "z+")
-    x_zm = send(x, "z-")
-    xy_zp = send(y_zp, "x")
+    x_z2 = send(z2[:, :edim], "x")
+    y_zp = send(y, "z+")
+    y_zm = send(y, "z-")
+    y_z2 = send(z2, "y")
+    x_zp = send(zp[:, :edim], "x")
+    x_zm = send(zm[:, :edim], "x")
+    xy_zp = send(xy, "z+")
+    xy_zm = send(xy, "z-")
     xy_z2 = send(x_z2, "y")
-    xy_zm = send(y_zm, "x")
     mine = [own, y, zp, y_zp, zm, y_zm, z2, y_z2]
     theirs = [x, xy, x_zp, xy_zp, x_zm, xy_zm, x_z2, xy_z2]
     prep = kernel_call(
         functools.partial(prep_kernel, edim),
-        in_specs=[VMEM, VMEM],
-        out_specs=(VMEM,) * 3,
-        out_shape=(local(rows, idim), local(idim // 2, idim // 2), local(idim // 2, idim // 2)),
-    )(near(ext), pivot)
+        in_specs=[HBM] * 3,
+        out_specs=(VMEM,) * 4,
+        out_shape=(
+            local(rows, idim),
+            local(idim // 2, idim // 2),
+            local(idim // 2, idim // 2),
+            pltpu.VMEM((rows, 128), F32),
+        ),
+        scratch_shapes=[
+            pltpu.VMEM((rows, idim), BF16),
+            pltpu.VMEM(pivot.shape, jnp.int32),
+            pltpu.SMEM(flags.shape, jnp.int32),
+            pltpu.SemaphoreType.DMA((3,)),
+        ],
+    )(distant(flags), distant(ext), distant(pivot))
     coupled, through = kernel_call(
         functools.partial(couple_kernel, edim),
-        in_specs=[SMEM] + [VMEM] * 11,
+        in_specs=[VMEM] * 12,
         out_specs=(VMEM,) * 2,
         out_shape=(local(rows, idim),) * 2,
-    )(flags, *map(near, prep), *map(near, mine))
-    out = product(through, mine, edim, ext=ext, flags=flags)
+    )(*map(near, prep), *map(near, mine))
+    out = product(through, mine, edim, ext=ext, sign=prep[-1])
     return product(coupled, theirs, edim, out=out)
 
 

time: 60.6 us -> 56.4 us (0.931)
  local copies, waits for them, and re-layouts: 6.21 us -> 0.07 us
  Pallas kernels: 13.3 us -> 14.8 us
    unnamed x12 -> x4, local copies, waits for them, and re-layouts: 6.21 us -> 0.01 us
    pallas_call x4, Pallas kernels: 3.44 us -> 6.14 us  [the longest x1 2.03 us: merge(): kernel_call(functools.partial(prep_kernel, edim), in_specs=[HBM] * 3, out...]
    pallas_call x2, Pallas kernels: 9.83 us -> 8.63 us  [product(): kernel_call(functools.partial(product_kernel, edim, 0 if own else edim, o...]
  transfers between devices with their start and end apart: 16 -> 16, of which waited for: 5 -> 6; matrix products, arithmetic and copies ran while one was open for 0% -> 0% of each run, Pallas kernels for 15% -> 17%
where the time goes in v1:
time: 56.4 us; the launch traced here: 56.2 us
  starting transfers between devices  28.9 us (51%)
  Pallas kernels  14.8 us (26%)
  waiting for transfers between devices  12.1 us (21%)
    ppermute x16, starting transfers between devices, send(): return lax.ppermute(array, ('leaf', 'panel'), ROUTES[name])  28.9 us
    ppermute x16, waiting for transfers between devices, send(): return lax.ppermute(array, ('leaf', 'panel'), ROUTES[name])  12.1 us
    pallas_call x2, Pallas kernels, product(): kernel_call(functools.partial(product_kernel, edim, 0 if own else edim, o...  8.63 us
    pallas_call x1, Pallas kernels, merge(): kernel_call(functools.partial(prep_kernel, edim), in_specs=[HBM] * 3, out...  2.03 us
    pallas_call x1, Pallas kernels, merge(): kernel_call(split_kernel, in_specs=[HBM] * 2, out_specs=(VMEM,) * 2, out_...  1.6 us
    pallas_call x1, Pallas kernels, merge(): kernel_call(inward_kernel, in_specs=[HBM], out_specs=VMEM, out_shape=loca...  1.29 us
    pallas_call x1, Pallas kernels, merge(): kernel_call(functools.partial(couple_kernel, edim), in_specs=[VMEM] * 12,...  1.21 us
  transfers between devices with their start and end apart: 16, of which 6 were waited for; matrix products, arithmetic and copies ran while one was open for 0% of the time, Pallas kernels for 17%

profile of v1, /device:TPU:0, one launch (start us, length us, event | category | flops | bytes accessed | tf_op | source)
XLA Modules:
  0.0 56.2 jit_solution(10486860137881123988)
XLA Ops:
  0.0 0.0 slice-start
  0.0 1.3 %shard_map.57 = bf16[32,512]{1,0:T(8,128)(2,1)S(1)} custom-call(bf16[64,5120]{1,0:T(8,128)(2,1)} %bitcast.8), custom_call_target="tpu_custom_call" | custom-call | tf_op jit(solution)/shard_map/pallas_call | solution.py:254
  1.3 1.7 %collective-permute-start = (bf16[32,512]{1,0:T(8,128)(2,1)S(1)}, bf16[32,512]{1,0:T(8,128)(2,1)S(1)}, u32[]{:S(2)}, u32[]{:S(2)}) collective-permute-start(bf16[32,512]{1,0:T(8,128)(2,1)S(1)} %shard_map.57), channel_id=1, source_target_pairs={{0,32},{8,40},{2,34},{10,42},{4,36},{12,44},{6,38},{14,46},{16,48}... | collective-permute-start | bytes 98312 | tf_op jit(solution)/shard_map/ppermute | solution.py:241
  3.0 1.6 %shard_map.56 = (bf16[32,4608]{1,0:T(8,128)(2,1)S(1)}, bf16[32,5632]{1,0:T(8,128)(2,1)S(1)}) custom-call(bf16[64,5120]{1,0:T(8,128)(2,1)} %bitcast.9, bf16[64,512]{1,0:T(8,128)(2,1)} %bitcast.10), custom_call_target="tpu_custom_call" | custom-call | tf_op jit(solution)/shard_map/pallas_call | solution.py:262
  4.6 0.7 %collective-permute-done = bf16[32,512]{1,0:T(8,128)(2,1)S(1)} collective-permute-done((bf16[32,512]{1,0:T(8,128)(2,1)S(1)}, bf16[32,512]{1,0:T(8,128)(2,1)S(1)}, u32[]{:S(2)}, u32[]{:S(2)}) %collective-permute-start) | collective-permute-done | bytes 32800 | tf_op jit(solution)/shard_map/ppermute | solution.py:241
  5.3 4.0 %collective-permute-start.6 = (bf16[32,5632]{1,0:T(8,128)(2,1)S(1)}, bf16[32,5632]{1,0:T(8,128)(2,1)S(1)}, u32[]{:S(2)}, u32[]{:S(2)}) collective-permute-start(bf16[32,5632]{1,0:T(8,128)(2,1)S(1)} %constant_dynamic-update-slice_fusion.rest_0_.refs_3_), channel_id=1, source_target_pairs={{0,4},{8,12},{2,6},{10,14},{4,0},{12,8},{6,2},{14,10},{16,20},{24,... | collective-permute-start | bytes 1081352 | tf_op jit(solution)/shard_map/ppermute | solution.py:241
  9.3 3.2 %collective-permute-start.1 = (bf16[32,5632]{1,0:T(8,128)(2,1)S(1)}, bf16[32,5632]{1,0:T(8,128)(2,1)S(1)}, u32[]{:S(2)}, u32[]{:S(2)}) collective-permute-start(bf16[32,5632]{1,0:T(8,128)(2,1)S(1)} %constant_dynamic-update-slice_fusion.rest_0_.refs_3_), channel_id=1, source_target_pairs={{0,1},{8,9},{2,3},{10,11},{4,5},{12,13},{6,7},{14,15},{16,17},{24,... | collective-permute-start | bytes 1081352 | tf_op jit(solution)/shard_map/ppermute | solution.py:241
  12.5 0.7 %collective-permute-start.4 = (bf16[32,5632]{1,0:T(8,128)(2,1)S(1)}, bf16[32,5632]{1,0:T(8,128)(2,1)S(1)}, u32[]{:S(2)}, u32[]{:S(2)}) collective-permute-start(bf16[32,5632]{1,0:T(8,128)(2,1)S(1)} %constant_dynamic-update-slice_fusion.rest_0_.refs_3_), channel_id=1, source_target_pairs={{0,6},{8,14},{2,0},{10,8},{4,2},{12,10},{6,4},{14,12},{16,22},{24,... | collective-permute-start | bytes 1081352 | tf_op jit(solution)/shard_map/ppermute | solution.py:241
  13.2 1.3 %collective-permute-start.2 = (bf16[32,5632]{1,0:T(8,128)(2,1)S(1)}, bf16[32,5632]{1,0:T(8,128)(2,1)S(1)}, u32[]{:S(2)}, u32[]{:S(2)}) collective-permute-start(bf16[32,5632]{1,0:T(8,128)(2,1)S(1)} %constant_dynamic-update-slice_fusion.rest_0_.refs_3_), channel_id=1, source_target_pairs={{0,2},{8,10},{2,4},{10,12},{4,6},{12,14},{6,0},{14,8},{16,18},{24,... | collective-permute-start | bytes 1081352 | tf_op jit(solution)/shard_map/ppermute | solution.py:241
  14.5 1.5 %collective-permute-start.8 = (bf16[32,4608]{1,0:T(8,128)(2,1)S(1)}, bf16[32,4608]{1,0:T(8,128)(2,1)S(1)}, u32[]{:S(2)}, u32[]{:S(2)}) collective-permute-start(bf16[32,4608]{1,0:T(8,128)(2,1)S(1)} %get-tuple-element.19), channel_id=1, source_target_pairs={{0,32},{8,40},{2,34},{10,42},{4,36},{12,44},{6,38},{14,46},{16,48}... | collective-permute-start | bytes 884744 | tf_op jit(solution)/shard_map/ppermute | solution.py:241
  16.0 2.6 %collective-permute-done.6.rest_6_.refs_9_ = bf16[32,5632]{1,0:T(8,128)(2,1)S(1)} collective-permute-done((bf16[32,5632]{1,0:T(8,128)(2,1)S(1)}, bf16[32,5632]{1,0:T(8,128)(2,1)S(1)}, u32[]{:S(2)}, u32[]{:S(2)}) %collective-permute-start.6) | collective-permute-done | bytes 360480 | tf_op jit(solution)/shard_map/ppermute | solution.py:241
  18.6 3.2 %collective-permute-start.7 = (bf16[32,5632]{1,0:T(8,128)(2,1)S(1)}, bf16[32,5632]{1,0:T(8,128)(2,1)S(1)}, u32[]{:S(2)}, u32[]{:S(2)}) collective-permute-start(bf16[32,5632]{1,0:T(8,128)(2,1)S(1)} %collective-permute-done.6.rest_6_.refs_9_), channel_id=1, source_target_pairs={{0,1},{8,9},{2,3},{10,11},{4,5},{12,13},{6,7},{14,15},{16,17},{24,... | collective-permute-start | bytes 1081352 | tf_op jit(solution)/shard_map/ppermute | solution.py:241
  21.8 0.0 collective-permute-done.1.rest_1_.refs_4_
  21.8 3.6 %collective-permute-start.5 = (bf16[32,5632]{1,0:T(8,128)(2,1)S(1)}, bf16[32,5632]{1,0:T(8,128)(2,1)S(1)}, u32[]{:S(2)}, u32[]{:S(2)}) collective-permute-start(bf16[32,5632]{1,0:T(8,128)(2,1)S(1)} %collective-permute-done.1.rest_1_.refs_4_), channel_id=1, source_target_pairs={{0,6},{8,14},{2,0},{10,8},{4,2},{12,10},{6,4},{14,12},{16,22},{24,... | collective-permute-start | bytes 1081352 | tf_op jit(solution)/shard_map/ppermute | solution.py:241
  25.4 0.0 collective-permute-done.8.refs_1_
  25.4 0.0 collective-permute-start.3
  25.5 1.9 %collective-permute-done.4.rest_4_.refs_7_ = bf16[32,5632]{1,0:T(8,128)(2,1)S(1)} collective-permute-done((bf16[32,5632]{1,0:T(8,128)(2,1)S(1)}, bf16[32,5632]{1,0:T(8,128)(2,1)S(1)}, u32[]{:S(2)}, u32[]{:S(2)}) %collective-permute-start.4) | collective-permute-done | bytes 360480 | tf_op jit(solution)/shard_map/ppermute | solution.py:241
  27.3 3.2 %collective-permute-start.9 = (bf16[32,4608]{1,0:T(8,128)(2,1)S(1)}, bf16[32,4608]{1,0:T(8,128)(2,1)S(1)}, u32[]{:S(2)}, u32[]{:S(2)}) collective-permute-start(bf16[32,4608]{1,0:T(8,128)(2,1)S(1)} %collective-permute-done.8.refs_1_), channel_id=1, source_target_pairs={{0,1},{8,9},{2,3},{10,11},{4,5},{12,13},{6,7},{14,15},{16,17},{24,... | collective-permute-start | bytes 884744 | tf_op jit(solution)/shard_map/ppermute | solution.py:241
  30.5 0.0 collective-permute-done.2.rest_2_.refs_5_
  30.5 1.5 %collective-permute-start.14 = (bf16[32,4608]{1,0:T(8,128)(2,1)S(1)}, bf16[32,4608]{1,0:T(8,128)(2,1)S(1)}, u32[]{:S(2)}, u32[]{:S(2)}) collective-permute-start(bf16[32,4608]{1,0:T(8,128)(2,1)S(1)} %slice.14), channel_id=1, source_target_pairs={{0,32},{8,40},{2,34},{10,42},{4,36},{12,44},{6,38},{14,46},{16,48}... | collective-permute-start | bytes 884744 | tf_op jit(solution)/shard_map/ppermute | solution.py:241
  32.0 3.5 %collective-permute-done.9.refs_2_ = bf16[32,4608]{1,0:T(8,128)(2,1)S(1)} collective-permute-done((bf16[32,4608]{1,0:T(8,128)(2,1)S(1)}, bf16[32,4608]{1,0:T(8,128)(2,1)S(1)}, u32[]{:S(2)}, u32[]{:S(2)}) %collective-permute-start.9) | collective-permute-done | bytes 294944 | tf_op jit(solution)/shard_map/ppermute | solution.py:241
  35.6 1.5 %collective-permute-start.12 = (bf16[32,4608]{1,0:T(8,128)(2,1)S(1)}, bf16[32,4608]{1,0:T(8,128)(2,1)S(1)}, u32[]{:S(2)}, u32[]{:S(2)}) collective-permute-start(bf16[32,4608]{1,0:T(8,128)(2,1)S(1)} %slice.13), channel_id=1, source_target_pairs={{0,32},{8,40},{2,34},{10,42},{4,36},{12,44},{6,38},{14,46},{16,48}... | collective-permute-start | bytes 884744 | tf_op jit(solution)/shard_map/ppermute | solution.py:241
  37.1 3.3 %collective-permute-done.14.refs_7_ = bf16[32,4608]{1,0:T(8,128)(2,1)S(1)} collective-permute-done((bf16[32,4608]{1,0:T(8,128)(2,1)S(1)}, bf16[32,4608]{1,0:T(8,128)(2,1)S(1)}, u32[]{:S(2)}, u32[]{:S(2)}) %collective-permute-start.14) | collective-permute-done | bytes 294944 | tf_op jit(solution)/shard_map/ppermute | solution.py:241
  40.4 1.5 %collective-permute-start.10 = (bf16[32,4608]{1,0:T(8,128)(2,1)S(1)}, bf16[32,4608]{1,0:T(8,128)(2,1)S(1)}, u32[]{:S(2)}, u32[]{:S(2)}) collective-permute-start(bf16[32,4608]{1,0:T(8,128)(2,1)S(1)} %slice.12), channel_id=1, source_target_pairs={{0,32},{8,40},{2,34},{10,42},{4,36},{12,44},{6,38},{14,46},{16,48}... | collective-permute-start | bytes 884744 | tf_op jit(solution)/shard_map/ppermute | solution.py:241
  41.9 0.0 collective-permute-done.7.rest_7_.refs_10_
  41.9 0.0 collective-permute-start.13
  41.9 0.0 collective-permute-done.5.rest_5_.refs_8_
  41.9 2.0 %collective-permute-start.11 = (bf16[32,4608]{1,0:T(8,128)(2,1)S(1)}, bf16[32,4608]{1,0:T(8,128)(2,1)S(1)}, u32[]{:S(2)}, u32[]{:S(2)}) collective-permute-start(bf16[32,4608]{1,0:T(8,128)(2,1)S(1)} %collective-permute-done.9.refs_2_), channel_id=1, source_target_pairs={{0,2},{8,10},{2,4},{10,12},{4,6},{12,14},{6,0},{14,8},{16,18},{24,... | collective-permute-start | bytes 884744 | tf_op jit(solution)/shard_map/ppermute | solution.py:241
  43.9 0.0 collective-permute-done.3.rest_3_.refs_6_
  43.9 0.0 collective-permute-start.15
  43.9 0.0 slice-start.1
  43.9 2.0 %shard_map.55 = (bf16[576,512]{1,0:T(8,128)(2,1)S(1)}, bf16[256,256]{1,0:T(8,128)(2,1)S(1)}, bf16[256,256]{1,0:T(8,128)(2,1)S(1)}, f32[576,128]{1,0:T(8,128)S(1)}) custom-call(s32[1,9]{1,0:T(1,128)} %flags_hbm.1, bf16[576,5120]{1,0:T(8,128)(2,1)} %bitcast.4, s32[1,256]{1,0:T(1,128)} %pivot_hbm.1), custom_call_target="tpu_custom_call" | custom-call | tf_op jit(solution)/shard_map/pallas_call | solution.py:291
  45.9 1.2 %shard_map.58 = (bf16[576,512]{1,0:T(8,128)(2,1)S(1)}, bf16[576,512]{1,0:T(8,128)(2,1)S(1)}) custom-call(bf16[576,512]{1,0:T(8,128)(2,1)S(1)} %get-tuple-element.13.across_ref, bf16[256,256]{1,0:T(8,128)(2,1)S(1)} %get-tuple-element.14.spread_ref, bf16[256,256]{1,0:T(8,128)(2,1)S(1)} %get-tuple-element.15.back_ref, ...), custom_call_target="tpu_custom_call" | custom-call | tf_op jit(solution)/shard_map/pallas_call | solution.py:308
  47.2 0.0 slice-done
  47.2 0.0 slice-done.1
  47.2 4.7 %shard_map.59.refs_9_ = bf16[576,9216]{1,0:T(8,128)(2,1)} custom-call(f32[576,128]{1,0:T(8,128)S(1)} %get-tuple-element.16.sign_ref.refs_0_, bf16[576,512]{1,0:T(8,128)(2,1)S(1)} %get-tuple-element.20.refs_1_, bf16[576,5120]{1,0:T(8,128)(2,1)S(1)} %bitcast.7, bf16[32,5632]{1,0:T(8,128)(2,1)S(1)} %constant_dynamic-update-slice_fusion.rest_0_.refs_3_, ...), custom_call_target="tpu_custom_call" | custom-call | flops 2717908992 | bytes 10616832 | tf_op jit(solution)/shard_map/pallas_call | solution.py:203
  51.9 0.0 collective-permute-done.12.refs_5_
  51.9 0.0 collective-permute-done.10.refs_3_
  51.9 0.0 collective-permute-done.13.refs_6_
  52.0 0.0 collective-permute-done.11.refs_4_
  52.0 0.2 collective-permute-done.15.refs_8_
  52.1 3.9 %shard_map.60 = bf16[576,9216]{1,0:T(8,128)(2,1)} custom-call(bf16[576,512]{1,0:T(8,128)(2,1)S(1)} %get-tuple-element.18.refs_0_, bf16[32,4608]{1,0:T(8,128)(2,1)S(1)} %collective-permute-done.8.refs_1_, bf16[32,4608]{1,0:T(8,128)(2,1)S(1)} %collective-permute-done.9.refs_2_, ...), custom_call_target="tpu_custom_call", output_to_operand_aliasing={{}: (9, {})} | custom-call | flops 2717908992 | bytes 10616832 | tf_op jit(solution)/shard_map/pallas_call | solution.py:203
  (5 shorter events, 0.1 us)
Async XLA Ops:
  0.0 47.2 %slice-start = ((s8[5898240]{0:T(1024)(128)(4,1)}), s8[4194304]{0:T(1024)(128)(4,1)S(1)}, s32[]{:S(2)}) async-start(s8[5898240]{0:T(1024)(128)(4,1)} %bitcast.5), calls=%async_computation | async-start | bytes 8388608
  1.3 4.0 %collective-permute-start = (bf16[32,512]{1,0:T(8,128)(2,1)S(1)}, bf16[32,512]{1,0:T(8,128)(2,1)S(1)}, u32[]{:S(2)}, u32[]{:S(2)}) collective-permute-start(bf16[32,512]{1,0:T(8,128)(2,1)S(1)} %shard_map.57), channel_id=1, source_target_pairs={{0,32},{8,40},{2,34},{10,42},{4,36},{12,44},{6,38},{14,46},{16,48}... | collective-permute-start | bytes 98312 | tf_op jit(solution)/shard_map/ppermute | solution.py:241
  5.3 13.3 %collective-permute-start.6 = (bf16[32,5632]{1,0:T(8,128)(2,1)S(1)}, bf16[32,5632]{1,0:T(8,128)(2,1)S(1)}, u32[]{:S(2)}, u32[]{:S(2)}) collective-permute-start(bf16[32,5632]{1,0:T(8,128)(2,1)S(1)} %constant_dynamic-update-slice_fusion.rest_0_.refs_3_), channel_id=1, source_target_pairs={{0,4},{8,12},{2,6},{10,14},{4,0},{12,8},{6,2},{14,10},{16,20},{24,... | collective-permute-start | bytes 1081352 | tf_op jit(solution)/shard_map/ppermute | solution.py:241
  9.3 12.5 %collective-permute-start.1 = (bf16[32,5632]{1,0:T(8,128)(2,1)S(1)}, bf16[32,5632]{1,0:T(8,128)(2,1)S(1)}, u32[]{:S(2)}, u32[]{:S(2)}) collective-permute-start(bf16[32,5632]{1,0:T(8,128)(2,1)S(1)} %constant_dynamic-update-slice_fusion.rest_0_.refs_3_), channel_id=1, source_target_pairs={{0,1},{8,9},{2,3},{10,11},{4,5},{12,13},{6,7},{14,15},{16,17},{24,... | collective-permute-start | bytes 1081352 | tf_op jit(solution)/shard_map/ppermute | solution.py:241
  12.5 14.8 %collective-permute-start.4 = (bf16[32,5632]{1,0:T(8,128)(2,1)S(1)}, bf16[32,5632]{1,0:T(8,128)(2,1)S(1)}, u32[]{:S(2)}, u32[]{:S(2)}) collective-permute-start(bf16[32,5632]{1,0:T(8,128)(2,1)S(1)} %constant_dynamic-update-slice_fusion.rest_0_.refs_3_), channel_id=1, source_target_pairs={{0,6},{8,14},{2,0},{10,8},{4,2},{12,10},{6,4},{14,12},{16,22},{24,... | collective-permute-start | bytes 1081352 | tf_op jit(solution)/shard_map/ppermute | solution.py:241
  13.2 17.3 %collective-permute-start.2 = (bf16[32,5632]{1,0:T(8,128)(2,1)S(1)}, bf16[32,5632]{1,0:T(8,128)(2,1)S(1)}, u32[]{:S(2)}, u32[]{:S(2)}) collective-permute-start(bf16[32,5632]{1,0:T(8,128)(2,1)S(1)} %constant_dynamic-update-slice_fusion.rest_0_.refs_3_), channel_id=1, source_target_pairs={{0,2},{8,10},{2,4},{10,12},{4,6},{12,14},{6,0},{14,8},{16,18},{24,... | collective-permute-start | bytes 1081352 | tf_op jit(solution)/shard_map/ppermute | solution.py:241
  14.5 10.9 %collective-permute-start.8 = (bf16[32,4608]{1,0:T(8,128)(2,1)S(1)}, bf16[32,4608]{1,0:T(8,128)(2,1)S(1)}, u32[]{:S(2)}, u32[]{:S(2)}) collective-permute-start(bf16[32,4608]{1,0:T(8,128)(2,1)S(1)} %get-tuple-element.19), channel_id=1, source_target_pairs={{0,32},{8,40},{2,34},{10,42},{4,36},{12,44},{6,38},{14,46},{16,48}... | collective-permute-start | bytes 884744 | tf_op jit(solution)/shard_map/ppermute | solution.py:241
  18.6 23.3 %collective-permute-start.7 = (bf16[32,5632]{1,0:T(8,128)(2,1)S(1)}, bf16[32,5632]{1,0:T(8,128)(2,1)S(1)}, u32[]{:S(2)}, u32[]{:S(2)}) collective-permute-start(bf16[32,5632]{1,0:T(8,128)(2,1)S(1)} %collective-permute-done.6.rest_6_.refs_9_), channel_id=1, source_target_pairs={{0,1},{8,9},{2,3},{10,11},{4,5},{12,13},{6,7},{14,15},{16,17},{24,... | collective-permute-start | bytes 1081352 | tf_op jit(solution)/shard_map/ppermute | solution.py:241
  21.8 20.1 %collective-permute-start.5 = (bf16[32,5632]{1,0:T(8,128)(2,1)S(1)}, bf16[32,5632]{1,0:T(8,128)(2,1)S(1)}, u32[]{:S(2)}, u32[]{:S(2)}) collective-permute-start(bf16[32,5632]{1,0:T(8,128)(2,1)S(1)} %collective-permute-done.1.rest_1_.refs_4_), channel_id=1, source_target_pairs={{0,6},{8,14},{2,0},{10,8},{4,2},{12,10},{6,4},{14,12},{16,22},{24,... | collective-permute-start | bytes 1081352 | tf_op jit(solution)/shard_map/ppermute | solution.py:241
  25.4 18.5 %collective-permute-start.3 = (bf16[32,5632]{1,0:T(8,128)(2,1)S(1)}, bf16[32,5632]{1,0:T(8,128)(2,1)S(1)}, u32[]{:S(2)}, u32[]{:S(2)}) collective-permute-start(bf16[32,5632]{1,0:T(8,128)(2,1)S(1)} %collective-permute-done.1.rest_1_.refs_4_), channel_id=1, source_target_pairs={{0,2},{8,10},{2,4},{10,12},{4,6},{12,14},{6,0},{14,8},{16,18},{24,... | collective-permute-start | bytes 1081352 | tf_op jit(solution)/shard_map/ppermute | solution.py:241
  27.3 8.2 %collective-permute-start.9 = (bf16[32,4608]{1,0:T(8,128)(2,1)S(1)}, bf16[32,4608]{1,0:T(8,128)(2,1)S(1)}, u32[]{:S(2)}, u32[]{:S(2)}) collective-permute-start(bf16[32,4608]{1,0:T(8,128)(2,1)S(1)} %collective-permute-done.8.refs_1_), channel_id=1, source_target_pairs={{0,1},{8,9},{2,3},{10,11},{4,5},{12,13},{6,7},{14,15},{16,17},{24,... | collective-permute-start | bytes 884744 | tf_op jit(solution)/shard_map/ppermute | solution.py:241
  30.5 9.9 %collective-permute-start.14 = (bf16[32,4608]{1,0:T(8,128)(2,1)S(1)}, bf16[32,4608]{1,0:T(8,128)(2,1)S(1)}, u32[]{:S(2)}, u32[]{:S(2)}) collective-permute-start(bf16[32,4608]{1,0:T(8,128)(2,1)S(1)} %slice.14), channel_id=1, source_target_pairs={{0,32},{8,40},{2,34},{10,42},{4,36},{12,44},{6,38},{14,46},{16,48}... | collective-permute-start | bytes 884744 | tf_op jit(solution)/shard_map/ppermute | solution.py:241
  35.6 16.4 %collective-permute-start.12 = (bf16[32,4608]{1,0:T(8,128)(2,1)S(1)}, bf16[32,4608]{1,0:T(8,128)(2,1)S(1)}, u32[]{:S(2)}, u32[]{:S(2)}) collective-permute-start(bf16[32,4608]{1,0:T(8,128)(2,1)S(1)} %slice.13), channel_id=1, source_target_pairs={{0,32},{8,40},{2,34},{10,42},{4,36},{12,44},{6,38},{14,46},{16,48}... | collective-permute-start | bytes 884744 | tf_op jit(solution)/shard_map/ppermute | solution.py:241
  40.4 11.6 %collective-permute-start.10 = (bf16[32,4608]{1,0:T(8,128)(2,1)S(1)}, bf16[32,4608]{1,0:T(8,128)(2,1)S(1)}, u32[]{:S(2)}, u32[]{:S(2)}) collective-permute-start(bf16[32,4608]{1,0:T(8,128)(2,1)S(1)} %slice.12), channel_id=1, source_target_pairs={{0,32},{8,40},{2,34},{10,42},{4,36},{12,44},{6,38},{14,46},{16,48}... | collective-permute-start | bytes 884744 | tf_op jit(solution)/shard_map/ppermute | solution.py:241
  41.9 10.1 %collective-permute-start.13 = (bf16[32,4608]{1,0:T(8,128)(2,1)S(1)}, bf16[32,4608]{1,0:T(8,128)(2,1)S(1)}, u32[]{:S(2)}, u32[]{:S(2)}) collective-permute-start(bf16[32,4608]{1,0:T(8,128)(2,1)S(1)} %collective-permute-done.9.refs_2_), channel_id=1, source_target_pairs={{0,6},{8,14},{2,0},{10,8},{4,2},{12,10},{6,4},{14,12},{16,22},{24,... | collective-permute-start | bytes 884744 | tf_op jit(solution)/shard_map/ppermute | solution.py:241
  41.9 10.1 %collective-permute-start.11 = (bf16[32,4608]{1,0:T(8,128)(2,1)S(1)}, bf16[32,4608]{1,0:T(8,128)(2,1)S(1)}, u32[]{:S(2)}, u32[]{:S(2)}) collective-permute-start(bf16[32,4608]{1,0:T(8,128)(2,1)S(1)} %collective-permute-done.9.refs_2_), channel_id=1, source_target_pairs={{0,2},{8,10},{2,4},{10,12},{4,6},{12,14},{6,0},{14,8},{16,18},{24,... | collective-permute-start | bytes 884744 | tf_op jit(solution)/shard_map/ppermute | solution.py:241
  43.9 8.2 %collective-permute-start.15 = (bf16[32,4608]{1,0:T(8,128)(2,1)S(1)}, bf16[32,4608]{1,0:T(8,128)(2,1)S(1)}, u32[]{:S(2)}, u32[]{:S(2)}) collective-permute-start(bf16[32,4608]{1,0:T(8,128)(2,1)S(1)} %collective-permute-done.14.refs_7_), channel_id=1, source_target_pairs={{0,1},{8,9},{2,3},{10,11},{4,5},{12,13},{6,7},{14,15},{16,17},{24,... | collective-permute-start | bytes 884744 | tf_op jit(solution)/shard_map/ppermute | solution.py:241
  43.9 3.3 %slice-start.1 = ((s8[5898240]{0:T(1024)(128)(4,1)}), s8[1703936]{0:T(1024)(128)(4,1)S(1)}, s32[]{:S(2)}) async-start(s8[5898240]{0:T(1024)(128)(4,1)} %bitcast.5), calls=%async_computation.1 | async-start | bytes 3407872
